TPU v7x, 128 devices: a whole 4x4x4 slice. The times are simulated.
128 devices in a mesh: grp: 2 (over z_hi), wid: 8 (over y, core), hid: 8 (over z_lo, x).
Axes of the slice: x: 4, y: 4, z: 4 (z_hi: 2, z_lo: 2; z = z_hi * 2 + z_lo), core: 2. Of those that a mesh axis runs over, the one named last changes fastest.
Arguments:
- student_in: bfloat16 [1024, 4096], P('wid'), may hold values from -6 to 6
- norm_gain: float32 [4096], replicated, may hold values from 0.1 to 1.9
- gate_weight: bfloat16 [4096, 7168], P(None, ('grp', 'hid')), may hold values from -0.09375 to 0.09375
- up_weight: bfloat16 [4096, 7168], P(None, ('grp', 'hid')), may hold values from -0.09375 to 0.09375
- down_weight: bfloat16 [7168, 4096], P(('grp', 'hid')), may hold values from -0.0625 to 0.0625
- projection: bfloat16 [4096, 8, 1024], P(None, None, ('grp', 'hid')), may hold values from -0.09375 to 0.09375
- teacher_in: bfloat16 [1024, 8192], P(None, 'wid'), may hold values from -6 to 6
- teacher_gate: bfloat16 [8192, 14336], P('wid', ('grp', 'hid')), may hold values from -0.0625 to 0.0625
- teacher_up: bfloat16 [8192, 14336], P('wid', ('grp', 'hid')), may hold values from -0.0625 to 0.0625
- teacher_down: bfloat16 [14336, 8192], P(('grp', 'hid'), 'wid'), may hold values from -0.046875 to 0.046875
Outputs:
- grad_gate: bfloat16 [4096, 7168], P('wid', ('grp', 'hid'))
- grad_up: bfloat16 [4096, 7168], P('wid', ('grp', 'hid'))
- grad_down: bfloat16 [7168, 4096], P(('grp', 'hid'), 'wid')
- grad_proj: bfloat16 [4096, 8, 1024], P('wid', None, ('grp', 'hid'))
- input_grad: float32 [1024, 4096], P('wid', ('grp', 'hid'))
All inputs are finite; a program needn't handle non-finite values.
Results may differ from a plain program's by a relative error of at most 0.02.
Values may be sent and summed in bfloat16 or wider, within the bound.
A program may use at most 128 MiB of HBM per device.

v0:
```python
import math
import jax
import jax.numpy as jnp
from jax import lax
from jax.sharding import Mesh
from jax.sharding import PartitionSpec as P

WID = ("wid_0", "wid_1")
GRP_HID = ("grp", "hid_0", "hid_1")


def split_up(array, dim, peers):
    shape = array.shape
    blocks = array.reshape(*shape[:dim], peers, shape[dim] // peers, *shape[dim + 1 :])
    return jnp.moveaxis(blocks, dim, 0)


def one_scatter(arrays, axis, dims):
    peers = lax.axis_size(axis)
    blocks = [split_up(a, dim, peers) for a, dim in zip(arrays, dims)]
    lines = jnp.concatenate([b.reshape(peers, -1) for b in blocks], axis=1)
    rows = max(16, -(-lines.shape[1] // 1024) * 8)
    lines = jnp.pad(lines, ((0, 0), (0, rows * 128 - lines.shape[1]))).reshape(-1, 128)
    vector, at, done = (lax.psum_scatter(lines, axis, tiled=True).reshape(-1), 0, [])
    for b in blocks:
        part = b[0]
        done.append(vector[at : at + part.size].reshape(part.shape))
        at += part.size
    return tuple(done)


def from_everyone(array, axis):
    peers = lax.axis_size(axis)
    return lax.all_to_all(
        jnp.broadcast_to(array[None], (peers, *array.shape)), axis, 0, 0, tiled=True
    )


def joined_along(blocks, dim):
    blocks = jnp.moveaxis(blocks, 0, dim)
    shape = blocks.shape
    return blocks.reshape(*shape[:dim], shape[dim] * shape[dim + 1], *shape[dim + 2 :])


def whole_of(array, axes, dim):
    far, near = axes
    blocks = from_everyone(from_everyone(array, far), near)
    return joined_along(blocks.swapaxes(0, 1).reshape(-1, *array.shape), dim)


def sent_and_summed(array, axis, dim):
    blocks = split_up(array, dim, lax.axis_size(axis))
    arrived = lax.all_to_all(blocks, axis, split_axis=0, concat_axis=0, tiled=True)
    return arrived.astype(jnp.float32).sum(axis=0)


def summed_rows(array, axes, dim):
    far, near = axes
    blocks = split_up(array, dim, lax.axis_size(far))
    nearer = sent_and_summed(blocks, near, dim + 1)
    arrived = lax.all_to_all(
        nearer.astype(jnp.bfloat16), far, split_axis=0, concat_axis=0, tiled=True
    )
    return arrived.astype(jnp.float32).sum(axis=0)


def rows_for(lines, peers):
    spare = -len(lines) % peers
    return jnp.pad(lines, [(0, spare)] + [(0, 0)] * (lines.ndim - 1))


def total_of(array, axes):
    lines = array.reshape(-1, array.shape[-1])
    own = summed_rows(rows_for(lines, lax.axis_size(axes[0]) * lax.axis_size(axes[1])), axes, 0)
    whole = whole_of(own.astype(jnp.bfloat16), axes, 0)
    return whole[: len(lines)].reshape(array.shape).astype(jnp.float32)


def of_everyone(array, axis):
    everything = from_everyone(array, axis)
    return jnp.sum(everything, axis=0)


def in_one_piece(arrays, axis, dim, along):
    ends, at = ([], 0)
    for a in arrays[:-1]:
        at += a.shape[along]
        ends.append(at)
    both = jnp.concatenate(arrays, axis=along)
    return tuple(jnp.split(lax.all_gather(both, axis, axis=dim, tiled=True), ends, axis=along))


def shards(
    student_in,
    norm_gain,
    gate_weight,
    up_weight,
    down_weight,
    projection,
    teacher_in,
    teacher_gate,
    teacher_up,
    teacher_down,
):
    f32 = jnp.float32
    bf16 = jnp.bfloat16
    gate_part = jnp.dot(teacher_in, teacher_gate, preferred_element_type=f32)
    up_part = jnp.dot(teacher_in, teacher_up, preferred_element_type=f32)
    gate_rows, up_rows = tuple(
        (
            part.astype(jnp.float32)
            for part in one_scatter(
                (gate_part.astype(jnp.bfloat16), up_part.astype(jnp.bfloat16)), WID, (0, 0)
            )
        )
    )
    teacher_hidden = (gate_rows * jax.nn.sigmoid(gate_rows) * up_rows).astype(bf16)
    feature_part = jnp.dot(
        whole_of(teacher_hidden, ("wid_0", "wid_1"), 0), teacher_down, preferred_element_type=f32
    )
    target_cols = (
        lax.psum_scatter(
            feature_part.astype(jnp.bfloat16), GRP_HID, scatter_dimension=1, tiled=True
        )
        .astype(jnp.float32)
        .astype(bf16)
    )
    target = lax.all_to_all(target_cols, WID, split_axis=0, concat_axis=1, tiled=True)
    tokens_dev = student_in.shape[0]
    width = student_in.shape[1]
    total_tokens = tokens_dev * lax.axis_size(WID)
    inputs = student_in.astype(f32)
    inverse_rms = lax.rsqrt(jnp.mean(inputs * inputs, axis=-1, keepdims=True) + 1e-05)
    normed = (inputs * inverse_rms * norm_gain).astype(bf16)
    gate_sum = jnp.dot(normed, gate_weight, preferred_element_type=f32)
    up_sum = jnp.dot(normed, up_weight, preferred_element_type=f32)
    sigma = jax.nn.sigmoid(gate_sum)
    hidden = (gate_sum * sigma * up_sum).astype(bf16)
    branch = total_of(
        jnp.dot(hidden, down_weight, preferred_element_type=f32).astype(jnp.bfloat16),
        ("grp", ("hid_0", "hid_1")),
    )
    summed = (inputs + branch).astype(bf16)
    proj_local = projection.reshape(width, -1)
    features = jnp.dot(summed, proj_local, preferred_element_type=f32)
    feature_error = ((features - target.astype(f32)) / math.sqrt(total_tokens)).astype(bf16)
    feature_grad = total_of(
        jnp.dot(feature_error, proj_local.T, preferred_element_type=f32).astype(jnp.bfloat16),
        ("grp", ("hid_0", "hid_1")),
    )
    branch_grad = feature_grad.astype(bf16)
    hidden_grad = jnp.dot(branch_grad, down_weight.T, preferred_element_type=f32)
    gate_grad = (hidden_grad * up_sum * sigma * (1.0 + gate_sum * (1.0 - sigma))).astype(bf16)
    up_grad = (hidden_grad * gate_sum * sigma).astype(bf16)
    normed_grad = jnp.dot(gate_grad, gate_weight.T, preferred_element_type=f32) + jnp.dot(
        up_grad, up_weight.T, preferred_element_type=f32
    )
    share_cols = width // lax.axis_size(GRP_HID)
    offset = lax.axis_index(GRP_HID) * share_cols
    normed_share = sent_and_summed(normed_grad.astype(jnp.bfloat16), GRP_HID, 1)
    input_share = lax.dynamic_slice_in_dim(inputs, offset, share_cols, 1)
    gain_share = lax.dynamic_slice_in_dim(norm_gain, offset, share_cols, 0)
    scaled = normed_share * gain_share
    moment = of_everyone(jnp.sum(scaled * input_share, axis=-1, keepdims=True), GRP_HID) / width
    grad_share = lax.dynamic_slice_in_dim(feature_grad, offset, share_cols, 1)
    input_grad = grad_share + inverse_rms * (
        scaled - input_share * inverse_rms * inverse_rms * moment
    )
    paired_grad = jnp.concatenate([gate_grad, up_grad], axis=1)
    summed_cols, branch_cols = (
        lax.all_to_all(summed, WID, split_axis=1, concat_axis=0, tiled=True),
        lax.all_to_all(branch_grad, WID, split_axis=1, concat_axis=0, tiled=True),
    )
    hidden_all, error_all = in_one_piece((hidden, feature_error), WID, 0, 1)
    weight_grad = lax.psum_scatter(
        jnp.dot(normed.T, paired_grad, preferred_element_type=f32).astype(jnp.bfloat16),
        WID,
        scatter_dimension=0,
        tiled=True,
    ).astype(jnp.float32)
    hidden_cols = gate_grad.shape[1]
    grad_gate = weight_grad[:, :hidden_cols].astype(bf16)
    grad_up = weight_grad[:, hidden_cols:].astype(bf16)
    grad_down = jnp.dot(hidden_all.T, branch_cols, preferred_element_type=f32).astype(bf16)
    grad_proj = jnp.dot(summed_cols.T, error_all, preferred_element_type=f32).astype(bf16)
    grad_proj = grad_proj.reshape(summed_cols.shape[1], lax.axis_size(WID), -1)
    return (grad_gate, grad_up, grad_down, grad_proj, input_grad)


def solution(mesh):
    split = Mesh(
        mesh.devices.reshape(mesh.shape["grp"], 4, 2, 2, 4),
        ("grp", "wid_0", "wid_1", "hid_0", "hid_1"),
    )
    in_specs = (
        P(WID, None),
        P(),
        P(None, GRP_HID),
        P(None, GRP_HID),
        P(GRP_HID, None),
        P(None, None, GRP_HID),
        P(None, WID),
        P(WID, GRP_HID),
        P(WID, GRP_HID),
        P(GRP_HID, WID),
    )
    out_specs = (
        P(WID, GRP_HID),
        P(WID, GRP_HID),
        P(GRP_HID, WID),
        P(WID, None, GRP_HID),
        P(WID, GRP_HID),
    )
    return jax.shard_map(
        shards, mesh=split, in_specs=in_specs, out_specs=out_specs, check_vma=False
    )
```

profile of v0, /device:TPU:1, one launch (start us, length us, event | category | flops | bytes accessed | tf_op | source)
XLA Modules:
  0.0 364.6 jit_solution(1658961827756413029)
XLA Ops:
  8.8 5.1 %convolution_convert_fusion.5 = bf16[1024,896]{1,0:T(8,128)(2,1)} fusion(bf16[1024,1024]{1,0:T(8,128)(2,1)S(1)} %copy-done, bf16[1024,896]{1,0:T(8,128)(2,1)} %param.17), kind=kOutput, calls=%fused_computation.13 | convolution fusion | flops 1879965696 | bytes 5767168 | tf_op jit(solution)/shard_map/dot_general | solution.py:107
  17.4 5.1 %convolution_convert_fusion.4 = bf16[1024,896]{1,0:T(8,128)(2,1)} fusion(bf16[1024,1024]{1,0:T(8,128)(2,1)S(1)} %copy-done, bf16[1024,896]{1,0:T(8,128)(2,1)} %param.18), kind=kOutput, calls=%fused_computation.12 | convolution fusion | flops 1879965696 | bytes 5767168 | tf_op jit(solution)/shard_map/dot_general | solution.py:108
  26.2 8.3 %pad_maximum_fusion = bf16[8,229376]{1,0:T(8,128)(2,1)} fusion(bf16[8,114688]{1,0:T(8,128)(2,1)} %reshape_reshape.21, bf16[8,114688]{1,0:T(8,128)(2,1)S(1)} %copy-done.3), kind=kLoop, calls=%fused_computation.5 | loop fusion | flops 7340032 | bytes 7340032 | tf_op jit(solution)/shard_map/concatenate | solution.py:21
  34.5 5.5 %reshape.88 = bf16[14336,128]{1,0:T(8,128)(2,1)} reshape(bf16[8,229376]{1,0:T(8,128)(2,1)} %pad_maximum_fusion) | data formatting | bytes 7340032 | tf_op jit(solution)/shard_map/reshape | solution.py:23
  40.1 37.3 %reduce-scatter.4.cloned.1.call-done = bf16[1792,128]{1,0:T(8,128)(2,1)} async-done(((bf16[14336,128]{1,0:T(8,128)(2,1)}), bf16[1792,128]{1,0:T(8,128)(2,1)}) %reduce-scatter.4.cloned.1.call-update) | async-done | bytes 458768 | tf_op jit(solution)/shard_map/reduce_scatter | solution.py:24
  79.9 4.9 %all-to-all-start.4 = ((bf16[4,128,896]{2,1,0:T(8,128)(2,1)}), bf16[4,128,896]{2,1,0:T(8,128)(2,1)S(1)}, u32[]{:S(2)}, u32[]{:S(2)}) async-start(bf16[4,128,896]{2,1,0:T(8,128)(2,1)} %broadcast_in_dim.16), calls=%async_computation.5 | async-start | bytes 1835008 | tf_op jit(solution)/shard_map/all_to_all | solution.py:34
  85.1 11.0 %all-to-all-done.4 = bf16[4,128,896]{2,1,0:T(8,128)(2,1)S(1)} async-done(((bf16[4,128,896]{2,1,0:T(8,128)(2,1)}), bf16[4,128,896]{2,1,0:T(8,128)(2,1)S(1)}, u32[]{:S(2)}, u32[]{:S(2)}) %all-to-all-start.4) | async-done | bytes 917536 | tf_op jit(solution)/shard_map/all_to_all | solution.py:34
  96.3 8.3 %all_to_all.111 = bf16[2,4,128,896]{3,2,1,0:T(8,128)(2,1)S(1)} all-to-all(bf16[2,4,128,896]{3,2,1,0:T(8,128)(2,1)S(1)} %broadcast_in_dim.17), channel_id=1, replica_groups=mesh['grp'=2,'wid_0'=4,'wid_1'=2,'hid_0'=2,'hid_1'=4] {'wid_1'}, dimensions={0} | all-to-all | bytes 3670016 | tf_op jit(solution)/shard_map/all_to_all | solution.py:34
  116.9 23.1 %all_to_all.112 = bf16[8,2,8,4096]{3,2,1,0:T(8,128)(2,1)S(1)} all-to-all(bf16[8,2,8,4096]{3,2,1,0:T(8,128)(2,1)S(1)} %bitcast.78), channel_id=1, replica_groups=mesh['grp'=2,'wid_0'=4,'wid_1'=2,'hid_0'=2,'hid_1'=4] {'hid_0','hid_1'}, dimensions={0} | all-to-all | bytes 2097152 | tf_op jit(solution)/shard_map/all_to_all | solution.py:53
  140.2 8.4 %all_to_all.113 = bf16[2,8,4096]{2,1,0:T(8,128)(2,1)S(1)} all-to-all(bf16[2,8,4096]{2,1,0:T(8,128)(2,1)S(1)} %reduce_sum.85), channel_id=1, replica_groups=mesh['grp'=2,'wid_0'=4,'wid_1'=2,'hid_0'=2,'hid_1'=4] {'grp'}, dimensions={0} | all-to-all | bytes 262144 | tf_op jit(solution)/shard_map/all_to_all | solution.py:61
  148.6 7.3 %all_to_all.114 = bf16[2,8,4096]{2,1,0:T(8,128)(2,1)S(1)} all-to-all(bf16[2,8,4096]{2,1,0:T(8,128)(2,1)S(1)} %broadcast_in_dim.14), channel_id=1, replica_groups=mesh['grp'=2,'wid_0'=4,'wid_1'=2,'hid_0'=2,'hid_1'=4] {'grp'}, dimensions={0} | all-to-all | bytes 262144 | tf_op jit(solution)/shard_map/all_to_all | solution.py:34
  160.7 15.1 %all-to-all-done.3 = bf16[8,2,8,4096]{3,2,1,0:T(8,128)(2,1)S(1)} async-done(((bf16[8,2,8,4096]{3,2,1,0:T(8,128)(2,1)}), bf16[8,2,8,4096]{3,2,1,0:T(8,128)(2,1)S(1)}, u32[]{:S(2)}, u32[]{:S(2)}) %all-to-all-start.3) | async-done | bytes 1048608 | tf_op jit(solution)/shard_map/all_to_all | solution.py:34
  177.3 13.6 %reduce-scatter.6.cloned.1.call-done = bf16[1024,64]{0,1:T(8,128)(2,1)} async-done(((bf16[1024,1024]{0,1:T(8,128)(2,1)}), bf16[1024,64]{0,1:T(8,128)(2,1)}) %reduce-scatter.6.cloned.1.call-update) | async-done | bytes 131088 | tf_op jit(solution)/shard_map/reduce_scatter | solution.py:122
  192.5 6.6 %all-to-all-start.6 = ((bf16[8,128,64]{1,2,0:T(8,128)(2,1)}), bf16[8,128,64]{1,2,0:T(8,128)(2,1)S(1)}, u32[]{:S(2)}, u32[]{:S(2)}) async-start(bf16[8,128,64]{1,2,0:T(8,128)(2,1)} %copy_bitcast_fusion.2), calls=%async_computation.8 | async-start | bytes 262144 | tf_op jit(solution)/shard_map/all_to_all | solution.py:128
  212.1 18.1 %all_to_all.115 = bf16[8,2,8,4096]{3,2,1,0:T(8,128)(2,1)S(1)} all-to-all(bf16[8,2,8,4096]{3,2,1,0:T(8,128)(2,1)S(1)} %bitcast.79), channel_id=1, replica_groups=mesh['grp'=2,'wid_0'=4,'wid_1'=2,'hid_0'=2,'hid_1'=4] {'hid_0','hid_1'}, dimensions={0} | all-to-all | bytes 2097152 | tf_op jit(solution)/shard_map/all_to_all | solution.py:53
  230.3 7.7 %all_to_all.116 = bf16[2,8,4096]{2,1,0:T(8,128)(2,1)S(1)} all-to-all(bf16[2,8,4096]{2,1,0:T(8,128)(2,1)S(1)} %reduce_sum.87), channel_id=1, replica_groups=mesh['grp'=2,'wid_0'=4,'wid_1'=2,'hid_0'=2,'hid_1'=4] {'grp'}, dimensions={0} | all-to-all | bytes 262144 | tf_op jit(solution)/shard_map/all_to_all | solution.py:61
  238.1 7.2 %all_to_all.117 = bf16[2,8,4096]{2,1,0:T(8,128)(2,1)S(1)} all-to-all(bf16[2,8,4096]{2,1,0:T(8,128)(2,1)S(1)} %broadcast_in_dim.18), channel_id=1, replica_groups=mesh['grp'=2,'wid_0'=4,'wid_1'=2,'hid_0'=2,'hid_1'=4] {'grp'}, dimensions={0} | all-to-all | bytes 262144 | tf_op jit(solution)/shard_map/all_to_all | solution.py:34
  245.5 14.4 %all_to_all.118 = bf16[8,2,8,4096]{3,2,1,0:T(8,128)(2,1)S(1)} all-to-all(bf16[8,2,8,4096]{3,2,1,0:T(8,128)(2,1)S(1)} %broadcast_in_dim.19), channel_id=1, replica_groups=mesh['grp'=2,'wid_0'=4,'wid_1'=2,'hid_0'=2,'hid_1'=4] {'hid_0','hid_1'}, dimensions={0} | all-to-all | bytes 2097152 | tf_op jit(solution)/shard_map/all_to_all | solution.py:34
  261.2 5.1 %convolution_convert_fusion = bf16[4096,896]{1,0:T(8,128)(2,1)} fusion(bf16[128,448]{0,1:T(8,128)(2,1)S(1)} %get-tuple-element.38, bf16[128,448]{0,1:T(8,128)(2,1)S(1)} %get-tuple-element.37, bf16[128,4096]{1,0:T(8,128)(2,1)S(1)} %copy-done.2, f32[4096]{0:T(1024)S(1)} %copy-done.9, f32[128]{0:T(128)S(1)} %add_rsqrt_fusion), kind=kOutput, calls=%fused_computation | convolution fusion | flops 945750016 | bytes 8634880 | tf_op jit(solution)/shard_map/dot_general | solution.py:176
  277.0 12.0 %all-to-all-done.13 = bf16[16,128,256]{2,1,0:T(8,128)(2,1)} async-done(((bf16[16,128,256]{2,1,0:T(8,128)(2,1)}), bf16[16,128,256]{2,1,0:T(8,128)(2,1)}, u32[]{:S(2)}, u32[]{:S(2)}) %all-to-all-start.13) | async-done | bytes 1048608 | tf_op jit(solution)/shard_map/all_to_all | solution.py:53
  289.0 9.0 %all-to-all-start.12 = ((bf16[128,8,512]{0,2,1:T(8,128)(2,1)}), bf16[128,8,512]{0,2,1:T(8,128)(2,1)S(1)}, u32[]{:S(2)}, u32[]{:S(2)}) async-start(bf16[128,8,512]{0,2,1:T(8,128)(2,1)} %bitcast.76), calls=%async_computation.15 | async-start | bytes 2097152 | tf_op jit(solution)/shard_map/all_to_all | solution.py:171
  302.0 17.0 %all-to-all-done.12 = bf16[128,8,512]{0,2,1:T(8,128)(2,1)S(1)} async-done(((bf16[128,8,512]{0,2,1:T(8,128)(2,1)}), bf16[128,8,512]{0,2,1:T(8,128)(2,1)S(1)}, u32[]{:S(2)}, u32[]{:S(2)}) %all-to-all-start.12) | async-done | bytes 1048608 | tf_op jit(solution)/shard_map/all_to_all | solution.py:171
  329.4 5.5 %all-to-all-start.11 = ((bf16[128,8,512]{2,0,1:T(8,128)(2,1)}), bf16[128,8,512]{2,0,1:T(8,128)(2,1)S(1)}, u32[]{:S(2)}, u32[]{:S(2)}) async-start(bf16[128,8,512]{2,0,1:T(8,128)(2,1)} %copy.64), calls=%async_computation.14 | async-start | bytes 2097152 | tf_op jit(solution)/shard_map/all_to_all | solution.py:172
  338.0 11.9 %all-to-all-done.11 = bf16[128,8,512]{2,0,1:T(8,128)(2,1)S(1)} async-done(((bf16[128,8,512]{2,0,1:T(8,128)(2,1)}), bf16[128,8,512]{2,0,1:T(8,128)(2,1)S(1)}, u32[]{:S(2)}, u32[]{:S(2)}) %all-to-all-start.11) | async-done | bytes 1048608 | tf_op jit(solution)/shard_map/all_to_all | solution.py:172
  (101 shorter events, 82.8 us)
Async XLA Ops:
  7.2 1.6 copy-start
  7.2 70.2 %reduce-scatter.4.cloned.1.call-start = ((), (), s32[]{:S(2)}) async-start(), calls=%async_computation.18 | async-start | bytes 4128768 | tf_op jit(solution)/shard_map/reduce_scatter | solution.py:24
  22.5 3.7 %copy-start.3 = (bf16[8,114688]{1,0:T(8,128)(2,1)S(1)}, bf16[8,114688]{1,0:T(8,128)(2,1)}, u32[]{:S(2)}) copy-start(bf16[8,114688]{1,0:T(8,128)(2,1)} %reshape_reshape.20) | copy-start | bytes 5505028
  78.7 6.1 %copy-start.2 = (bf16[128,4096]{1,0:T(8,128)(2,1)S(1)}, bf16[128,4096]{1,0:T(8,128)(2,1)}, u32[]{:S(2)}) copy-start(bf16[128,4096]{1,0:T(8,128)(2,1)} %param.10) | copy-start | bytes 3145732
  79.9 16.2 %all-to-all-start.4 = ((bf16[4,128,896]{2,1,0:T(8,128)(2,1)}), bf16[4,128,896]{2,1,0:T(8,128)(2,1)S(1)}, u32[]{:S(2)}, u32[]{:S(2)}) async-start(bf16[4,128,896]{2,1,0:T(8,128)(2,1)} %broadcast_in_dim.16), calls=%async_computation.5 | async-start | bytes 1835008 | tf_op jit(solution)/shard_map/all_to_all | solution.py:34
  84.8 106.1 %reduce-scatter.6.cloned.1.call-start = ((), (), s32[]{:S(2)}) async-start(), calls=%async_computation.19 | async-start | bytes 2228224 | tf_op jit(solution)/shard_map/reduce_scatter | solution.py:122
  110.5 3.4 copy-start.6
  113.9 1.9 copy-start.12
  113.9 2.1 copy-start.4
  157.0 18.8 %all-to-all-start.3 = ((bf16[8,2,8,4096]{3,2,1,0:T(8,128)(2,1)}), bf16[8,2,8,4096]{3,2,1,0:T(8,128)(2,1)S(1)}, u32[]{:S(2)}, u32[]{:S(2)}) async-start(bf16[8,2,8,4096]{3,2,1,0:T(8,128)(2,1)} %broadcast_in_dim.15), calls=%async_computation.3 | async-start | bytes 2097152 | tf_op jit(solution)/shard_map/all_to_all | solution.py:34
  192.5 11.8 %all-to-all-start.6 = ((bf16[8,128,64]{1,2,0:T(8,128)(2,1)}), bf16[8,128,64]{1,2,0:T(8,128)(2,1)S(1)}, u32[]{:S(2)}, u32[]{:S(2)}) async-start(bf16[8,128,64]{1,2,0:T(8,128)(2,1)} %copy_bitcast_fusion.2), calls=%async_computation.8 | async-start | bytes 262144 | tf_op jit(solution)/shard_map/all_to_all | solution.py:128
  199.1 150.9 %all-gather.2.cloned.1.call-start = ((), (), s32[]{:S(2)}) async-start(), calls=%async_computation.21 | async-start | bytes 2359296 | tf_op jit(solution)/shard_map/all_gather | solution.py:90
  209.0 145.6 %reduce-scatter.8.cloned.1.call-start = ((), (), s32[]{:S(2)}) async-start(), calls=%async_computation.20 | async-start | bytes 8257536 | tf_op jit(solution)/shard_map/reduce_scatter | solution.py:175
  245.4 14.6 %copy-start.5 = (bf16[448,4096]{1,0:T(8,128)(2,1)S(1)}, bf16[448,4096]{1,0:T(8,128)(2,1)}, u32[]{:S(2)}) copy-start(bf16[448,4096]{1,0:T(8,128)(2,1)} %param.14) | copy-start | bytes 11010052
  245.4 14.6 %copy-start.13 = (f32[128,448]{0,1:T(8,128)S(1)}, f32[128,448]{0,1:T(8,128)}, u32[]{:S(2)}) copy-start(f32[128,448]{0,1:T(8,128)} %copy-done.12) | copy-start | bytes 688132
  245.4 14.6 %copy-start.14 = (f32[128,448]{0,1:T(8,128)S(1)}, f32[128,448]{0,1:T(8,128)}, u32[]{:S(2)}) copy-start(f32[128,448]{0,1:T(8,128)} %get-tuple-element.42) | copy-start | bytes 688132
  266.3 3.1 copy-start.7
  271.3 17.7 %all-to-all-start.13 = ((bf16[16,128,256]{2,1,0:T(8,128)(2,1)}), bf16[16,128,256]{2,1,0:T(8,128)(2,1)}, u32[]{:S(2)}, u32[]{:S(2)}) async-start(bf16[16,128,256]{2,1,0:T(8,128)(2,1)} %bitcast.77), calls=%async_computation.16 | async-start | bytes 2097152 | tf_op jit(solution)/shard_map/all_to_all | solution.py:53
  289.0 30.0 %all-to-all-start.12 = ((bf16[128,8,512]{0,2,1:T(8,128)(2,1)}), bf16[128,8,512]{0,2,1:T(8,128)(2,1)S(1)}, u32[]{:S(2)}, u32[]{:S(2)}) async-start(bf16[128,8,512]{0,2,1:T(8,128)(2,1)} %bitcast.76), calls=%async_computation.15 | async-start | bytes 2097152 | tf_op jit(solution)/shard_map/all_to_all | solution.py:171
  319.6 9.8 %all-to-all-start.14 = ((f32[16,128,1]{1,2,0:T(1,128)}), f32[16,128,1]{1,2,0:T(1,128)S(1)}, u32[]{:S(2)}, u32[]{:S(2)}) async-start(f32[16,128,1]{1,2,0:T(1,128)} %broadcast_in_dim.20), calls=%async_computation.17 | async-start | bytes 16384 | tf_op jit(solution)/shard_map/all_to_all | solution.py:34
  329.4 20.5 %all-to-all-start.11 = ((bf16[128,8,512]{2,0,1:T(8,128)(2,1)}), bf16[128,8,512]{2,0,1:T(8,128)(2,1)S(1)}, u32[]{:S(2)}, u32[]{:S(2)}) async-start(bf16[128,8,512]{2,0,1:T(8,128)(2,1)} %copy.64), calls=%async_computation.14 | async-start | bytes 2097152 | tf_op jit(solution)/shard_map/all_to_all | solution.py:172
  338.0 14.8 %copy-start.8 = (bf16[8,128,512]{2,1,0:T(8,128)(2,1)S(1)}, bf16[8,128,512]{2,1,0:T(8,128)(2,1)}, u32[]{:S(2)}) copy-start(bf16[8,128,512]{2,1,0:T(8,128)(2,1)} %copy.66) | copy-start | bytes 3145732
  349.9 2.8 copy-start.10
  352.8 5.3 %copy-start.1 = (bf16[1024,1024]{1,0:T(8,128)(2,1)S(1)}, bf16[1024,1024]{1,0:T(8,128)(2,1)}, u32[]{:S(2)}) copy-start(bf16[1024,1024]{1,0:T(8,128)(2,1)} %param.16) | copy-start | bytes 6291460
  (2 other events, 2.2 us)
Sparse Core Ops, SparseCore 0:
  40.2 37.1 reduce-scatter.3
  110.0 80.8 reduce-scatter.5
  209.2 23.2 all-gather.1
  266.4 57.8 reduce-scatter.7
where the time goes:
time: 366 us; the launch traced here: 365 us
  waiting for transfers between devices  126 us (34%)
  blocking collectives  94.6 us (26%)
  matrix products  41.1 us (11%)
  starting transfers between devices  37.5 us (10%)
  local copies, waits for them, and re-layouts  31.3 us (9%)
  other arithmetic  20 us (5%)
  between operations  14.1 us (4%)
    all_to_all x2, blocking collectives, sent_and_summed(): lax.all_to_all(blocks, axis, split_axis=0, concat_axis=0, tiled=True)  41.2 us
    reduce_scatter x1, waiting for transfers between devices, one_scatter(): lax.psum_scatter(lines, axis, tiled=True).reshape(-1)  37.3 us
    all_to_all x4, blocking collectives, from_everyone(): lax.all_to_all(jnp.broadcast_to(array[None], (peers, *array.shape)), axis...  37.2 us
    all_to_all x3, waiting for transfers between devices, from_everyone(): lax.all_to_all(jnp.broadcast_to(array[None], (peers, *array.shape)), axis...  30.7 us
    all_to_all x1, waiting for transfers between devices, shards(): lax.all_to_all(summed, WID, split_axis=1, concat_axis=0, tiled=True)  17 us
    all_to_all x2, blocking collectives, summed_rows(): lax.all_to_all(nearer.astype(jnp.bfloat16), far, split_axis=0, concat_axi...  16.1 us
    reduce_scatter x1, waiting for transfers between devices, shards(): lax.psum_scatter(feature_part.astype(jnp.bfloat16), GRP_HID, scatter_dime...  13.6 us
    all_to_all x1, waiting for transfers between devices, sent_and_summed(): lax.all_to_all(blocks, axis, split_axis=0, concat_axis=0, tiled=True)  12 us
  transfers between devices with their start and end apart: 11, of which 9 were waited for; matrix products, arithmetic and copies ran while one was open for 11% of the time, Pallas kernels for 0%

commit v1 on v0

--- a/solution.py
+++ b/solution.py
@@ -169,7 +169,12 @@
     paired_grad = jnp.concatenate([gate_grad, up_grad], axis=1)
     summed_cols, branch_cols = (
         lax.all_to_all(summed, WID, split_axis=1, concat_axis=0, tiled=True),
-        lax.all_to_all(branch_grad, WID, split_axis=1, concat_axis=0, tiled=True),
+        jnp.concatenate(
+            lax.all_to_all(
+                jnp.stack(jnp.split(branch_grad, lax.axis_size(WID), axis=1)), WID, 0, 0
+            ),
+            axis=0,
+        ),
     )
     hidden_all, error_all = in_one_piece((hidden, feature_error), WID, 0, 1)
     weight_grad = lax.psum_scatter(

time: 366 us -> 367 us (level)
  waiting for transfers between devices: 126 us -> 122 us
    all_to_all x1, waiting for transfers between devices: 12 us -> 7.75 us  [sent_and_summed(): lax.all_to_all(blocks, axis, split_axis=0, concat_axis=0, tiled=True)]
    unnamed x33 -> x39, local copies, waits for them, and re-layouts: 6.35 us -> 10.6 us
  transfers between devices with their start and end apart: 11 -> 11, of which waited for: 9 -> 9; matrix products, arithmetic and copies ran while one was open for 11% -> 12% of each run, Pallas kernels for 0% -> 0%
where the time goes in v1:
time: 367 us; the launch traced here: 366 us
  waiting for transfers between devices  122 us (33%)
  blocking collectives  94.6 us (26%)
  matrix products  41.5 us (11%)
  starting transfers between devices  38.2 us (10%)
  local copies, waits for them, and re-layouts  34.9 us (10%)
  other arithmetic  20 us (5%)
  between operations  14.1 us (4%)
    all_to_all x2, blocking collectives, sent_and_summed(): lax.all_to_all(blocks, axis, split_axis=0, concat_axis=0, tiled=True)  41.2 us
    reduce_scatter x1, waiting for transfers between devices, one_scatter(): lax.psum_scatter(lines, axis, tiled=True).reshape(-1)  37.3 us
    all_to_all x4, blocking collectives, from_everyone(): lax.all_to_all(jnp.broadcast_to(array[None], (peers, *array.shape)), axis...  37.2 us
    all_to_all x3, waiting for transfers between devices, from_everyone(): lax.all_to_all(jnp.broadcast_to(array[None], (peers, *array.shape)), axis...  31.7 us
    all_to_all x1, waiting for transfers between devices, shards(): lax.all_to_all(summed, WID, split_axis=1, concat_axis=0, tiled=True)  16.6 us
    all_to_all x2, blocking collectives, summed_rows(): lax.all_to_all(nearer.astype(jnp.bfloat16), far, split_axis=0, concat_axi...  16.1 us
    reduce_scatter x1, waiting for transfers between devices, shards(): lax.psum_scatter(feature_part.astype(jnp.bfloat16), GRP_HID, scatter_dime...  13.6 us
    all_to_all x1, waiting for transfers between devices, shards(): lax.all_to_all(jnp.stack(jnp.split(branch_grad, lax.axis_size(WID), axis=...  12 us
  transfers between devices with their start and end apart: 11, of which 9 were waited for; matrix products, arithmetic and copies ran while one was open for 12% of the time, Pallas kernels for 0%

profile of v1, /device:TPU:1, one launch (start us, length us, event | category | flops | bytes accessed | tf_op | source)
XLA Modules:
  0.0 365.7 jit_solution(3240365311254828148)
XLA Ops:
  8.8 5.1 %convolution_convert_fusion.5 = bf16[1024,896]{1,0:T(8,128)(2,1)} fusion(bf16[1024,1024]{1,0:T(8,128)(2,1)S(1)} %copy-done, bf16[1024,896]{1,0:T(8,128)(2,1)} %param.17), kind=kOutput, calls=%fused_computation.13 | convolution fusion | flops 1879965696 | bytes 5767168 | tf_op jit(solution)/shard_map/dot_general | solution.py:107
  17.4 5.1 %convolution_convert_fusion.4 = bf16[1024,896]{1,0:T(8,128)(2,1)} fusion(bf16[1024,1024]{1,0:T(8,128)(2,1)S(1)} %copy-done, bf16[1024,896]{1,0:T(8,128)(2,1)} %param.18), kind=kOutput, calls=%fused_computation.12 | convolution fusion | flops 1879965696 | bytes 5767168 | tf_op jit(solution)/shard_map/dot_general | solution.py:108
  26.2 8.3 %pad_maximum_fusion = bf16[8,229376]{1,0:T(8,128)(2,1)} fusion(bf16[8,114688]{1,0:T(8,128)(2,1)} %reshape_reshape.21, bf16[8,114688]{1,0:T(8,128)(2,1)S(1)} %copy-done.3), kind=kLoop, calls=%fused_computation.5 | loop fusion | flops 7340032 | bytes 7340032 | tf_op jit(solution)/shard_map/concatenate | solution.py:21
  34.5 5.5 %reshape.87 = bf16[14336,128]{1,0:T(8,128)(2,1)} reshape(bf16[8,229376]{1,0:T(8,128)(2,1)} %pad_maximum_fusion) | data formatting | bytes 7340032 | tf_op jit(solution)/shard_map/reshape | solution.py:23
  40.1 37.3 %reduce-scatter.4.cloned.1.call-done = bf16[1792,128]{1,0:T(8,128)(2,1)} async-done(((bf16[14336,128]{1,0:T(8,128)(2,1)}), bf16[1792,128]{1,0:T(8,128)(2,1)}) %reduce-scatter.4.cloned.1.call-update) | async-done | bytes 458768 | tf_op jit(solution)/shard_map/reduce_scatter | solution.py:24
  85.1 11.0 %all-to-all-done.4 = bf16[4,128,896]{2,1,0:T(8,128)(2,1)S(1)} async-done(((bf16[4,128,896]{2,1,0:T(8,128)(2,1)}), bf16[4,128,896]{2,1,0:T(8,128)(2,1)S(1)}, u32[]{:S(2)}, u32[]{:S(2)}) %all-to-all-start.4) | async-done | bytes 917536 | tf_op jit(solution)/shard_map/all_to_all | solution.py:34
  96.3 8.3 %all_to_all.97 = bf16[2,4,128,896]{3,2,1,0:T(8,128)(2,1)S(1)} all-to-all(bf16[2,4,128,896]{3,2,1,0:T(8,128)(2,1)S(1)} %broadcast_in_dim.17), channel_id=1, replica_groups=mesh['grp'=2,'wid_0'=4,'wid_1'=2,'hid_0'=2,'hid_1'=4] {'wid_1'}, dimensions={0} | all-to-all | bytes 3670016 | tf_op jit(solution)/shard_map/all_to_all | solution.py:34
  116.9 23.1 %all_to_all.98 = bf16[8,2,8,4096]{3,2,1,0:T(8,128)(2,1)S(1)} all-to-all(bf16[8,2,8,4096]{3,2,1,0:T(8,128)(2,1)S(1)} %bitcast.111), channel_id=1, replica_groups=mesh['grp'=2,'wid_0'=4,'wid_1'=2,'hid_0'=2,'hid_1'=4] {'hid_0','hid_1'}, dimensions={0} | all-to-all | bytes 2097152 | tf_op jit(solution)/shard_map/all_to_all | solution.py:53
  140.2 8.4 %all_to_all.99 = bf16[2,8,4096]{2,1,0:T(8,128)(2,1)S(1)} all-to-all(bf16[2,8,4096]{2,1,0:T(8,128)(2,1)S(1)} %reduce_sum.85), channel_id=1, replica_groups=mesh['grp'=2,'wid_0'=4,'wid_1'=2,'hid_0'=2,'hid_1'=4] {'grp'}, dimensions={0} | all-to-all | bytes 262144 | tf_op jit(solution)/shard_map/all_to_all | solution.py:61
  148.6 7.3 %all_to_all.100 = bf16[2,8,4096]{2,1,0:T(8,128)(2,1)S(1)} all-to-all(bf16[2,8,4096]{2,1,0:T(8,128)(2,1)S(1)} %broadcast_in_dim.14), channel_id=1, replica_groups=mesh['grp'=2,'wid_0'=4,'wid_1'=2,'hid_0'=2,'hid_1'=4] {'grp'}, dimensions={0} | all-to-all | bytes 262144 | tf_op jit(solution)/shard_map/all_to_all | solution.py:34
  160.7 15.1 %all-to-all-done.3 = bf16[8,2,8,4096]{3,2,1,0:T(8,128)(2,1)S(1)} async-done(((bf16[8,2,8,4096]{3,2,1,0:T(8,128)(2,1)}), bf16[8,2,8,4096]{3,2,1,0:T(8,128)(2,1)S(1)}, u32[]{:S(2)}, u32[]{:S(2)}) %all-to-all-start.3) | async-done | bytes 1048608 | tf_op jit(solution)/shard_map/all_to_all | solution.py:34
  177.3 13.6 %reduce-scatter.6.cloned.1.call-done = bf16[1024,64]{0,1:T(8,128)(2,1)} async-done(((bf16[1024,1024]{0,1:T(8,128)(2,1)}), bf16[1024,64]{0,1:T(8,128)(2,1)}) %reduce-scatter.6.cloned.1.call-update) | async-done | bytes 131088 | tf_op jit(solution)/shard_map/reduce_scatter | solution.py:122
  192.5 6.6 %all-to-all-start.6 = ((bf16[8,128,64]{1,2,0:T(8,128)(2,1)}), bf16[8,128,64]{1,2,0:T(8,128)(2,1)S(1)}, u32[]{:S(2)}, u32[]{:S(2)}) async-start(bf16[8,128,64]{1,2,0:T(8,128)(2,1)} %copy_bitcast_fusion.2), calls=%async_computation.8 | async-start | bytes 262144 | tf_op jit(solution)/shard_map/all_to_all | solution.py:128
  212.1 18.1 %all_to_all.101 = bf16[8,2,8,4096]{3,2,1,0:T(8,128)(2,1)S(1)} all-to-all(bf16[8,2,8,4096]{3,2,1,0:T(8,128)(2,1)S(1)} %bitcast.112), channel_id=1, replica_groups=mesh['grp'=2,'wid_0'=4,'wid_1'=2,'hid_0'=2,'hid_1'=4] {'hid_0','hid_1'}, dimensions={0} | all-to-all | bytes 2097152 | tf_op jit(solution)/shard_map/all_to_all | solution.py:53
  230.3 7.7 %all_to_all.102 = bf16[2,8,4096]{2,1,0:T(8,128)(2,1)S(1)} all-to-all(bf16[2,8,4096]{2,1,0:T(8,128)(2,1)S(1)} %reduce_sum.87), channel_id=1, replica_groups=mesh['grp'=2,'wid_0'=4,'wid_1'=2,'hid_0'=2,'hid_1'=4] {'grp'}, dimensions={0} | all-to-all | bytes 262144 | tf_op jit(solution)/shard_map/all_to_all | solution.py:61
  238.1 7.2 %all_to_all.103 = bf16[2,8,4096]{2,1,0:T(8,128)(2,1)S(1)} all-to-all(bf16[2,8,4096]{2,1,0:T(8,128)(2,1)S(1)} %broadcast_in_dim.18), channel_id=1, replica_groups=mesh['grp'=2,'wid_0'=4,'wid_1'=2,'hid_0'=2,'hid_1'=4] {'grp'}, dimensions={0} | all-to-all | bytes 262144 | tf_op jit(solution)/shard_map/all_to_all | solution.py:34
  245.5 14.4 %all_to_all.104 = bf16[8,2,8,4096]{3,2,1,0:T(8,128)(2,1)S(1)} all-to-all(bf16[8,2,8,4096]{3,2,1,0:T(8,128)(2,1)S(1)} %broadcast_in_dim.19), channel_id=1, replica_groups=mesh['grp'=2,'wid_0'=4,'wid_1'=2,'hid_0'=2,'hid_1'=4] {'hid_0','hid_1'}, dimensions={0} | all-to-all | bytes 2097152 | tf_op jit(solution)/shard_map/all_to_all | solution.py:34
  261.2 5.1 %convolution_convert_fusion = bf16[4096,896]{1,0:T(8,128)(2,1)} fusion(bf16[128,448]{0,1:T(8,128)(2,1)S(1)} %get-tuple-element.38, bf16[128,448]{0,1:T(8,128)(2,1)S(1)} %get-tuple-element.37, bf16[128,4096]{1,0:T(8,128)(2,1)S(1)} %copy-done.2, f32[4096]{0:T(1024)S(1)} %copy-done.9, f32[128]{0:T(128)S(1)} %add_rsqrt_fusion), kind=kOutput, calls=%fused_computation | convolution fusion | flops 945750016 | bytes 8634880 | tf_op jit(solution)/shard_map/dot_general | solution.py:181
  281.3 7.7 %all-to-all-done.13 = bf16[16,128,256]{2,1,0:T(8,128)(2,1)} async-done(((bf16[16,128,256]{2,1,0:T(8,128)(2,1)}), bf16[16,128,256]{2,1,0:T(8,128)(2,1)}, u32[]{:S(2)}, u32[]{:S(2)}) %all-to-all-start.13) | async-done | bytes 1048608 | tf_op jit(solution)/shard_map/all_to_all | solution.py:53
  289.0 9.0 %all-to-all-start.12 = ((bf16[128,8,512]{0,2,1:T(8,128)(2,1)}), bf16[128,8,512]{0,2,1:T(8,128)(2,1)S(1)}, u32[]{:S(2)}, u32[]{:S(2)}) async-start(bf16[128,8,512]{0,2,1:T(8,128)(2,1)} %bitcast.110), calls=%async_computation.15 | async-start | bytes 2097152 | tf_op jit(solution)/shard_map/all_to_all | solution.py:171
  302.5 16.6 %all-to-all-done.12 = bf16[128,8,512]{0,2,1:T(8,128)(2,1)S(1)} async-done(((bf16[128,8,512]{0,2,1:T(8,128)(2,1)}), bf16[128,8,512]{0,2,1:T(8,128)(2,1)S(1)}, u32[]{:S(2)}, u32[]{:S(2)}) %all-to-all-start.12) | async-done | bytes 1048608 | tf_op jit(solution)/shard_map/all_to_all | solution.py:171
  323.8 5.6 %all-to-all-done.14 = f32[16,128,1]{1,2,0:T(1,128)S(1)} async-done(((f32[16,128,1]{1,2,0:T(1,128)}), f32[16,128,1]{1,2,0:T(1,128)S(1)}, u32[]{:S(2)}, u32[]{:S(2)}) %all-to-all-start.14) | async-done | bytes 8224 | tf_op jit(solution)/shard_map/all_to_all | solution.py:34
  329.4 6.2 %all-to-all-start.11 = ((bf16[8,128,512]{2,1,0:T(8,128)(2,1)}), bf16[8,128,512]{2,1,0:T(8,128)(2,1)}, u32[]{:S(2)}, u32[]{:S(2)}) async-start(bf16[8,128,512]{2,1,0:T(8,128)(2,1)} %fusion.9), calls=%async_computation.14 | async-start | bytes 2097152 | tf_op jit(solution)/shard_map/all_to_all | solution.py:173
  338.7 12.0 %all-to-all-done.11 = bf16[8,128,512]{2,1,0:T(8,128)(2,1)} async-done(((bf16[8,128,512]{2,1,0:T(8,128)(2,1)}), bf16[8,128,512]{2,1,0:T(8,128)(2,1)}, u32[]{:S(2)}, u32[]{:S(2)}) %all-to-all-start.11) | async-done | bytes 1048608 | tf_op jit(solution)/shard_map/all_to_all | solution.py:173
  (107 shorter events, 87.2 us)
Async XLA Ops:
  7.2 1.6 copy-start
  7.2 70.2 %reduce-scatter.4.cloned.1.call-start = ((), (), s32[]{:S(2)}) async-start(), calls=%async_computation.18 | async-start | bytes 4128768 | tf_op jit(solution)/shard_map/reduce_scatter | solution.py:24
  22.5 3.7 %copy-start.3 = (bf16[8,114688]{1,0:T(8,128)(2,1)S(1)}, bf16[8,114688]{1,0:T(8,128)(2,1)}, u32[]{:S(2)}) copy-start(bf16[8,114688]{1,0:T(8,128)(2,1)} %reshape_reshape.20) | copy-start | bytes 5505028
  78.7 6.1 %copy-start.2 = (bf16[128,4096]{1,0:T(8,128)(2,1)S(1)}, bf16[128,4096]{1,0:T(8,128)(2,1)}, u32[]{:S(2)}) copy-start(bf16[128,4096]{1,0:T(8,128)(2,1)} %param.10) | copy-start | bytes 3145732
  79.9 16.2 %all-to-all-start.4 = ((bf16[4,128,896]{2,1,0:T(8,128)(2,1)}), bf16[4,128,896]{2,1,0:T(8,128)(2,1)S(1)}, u32[]{:S(2)}, u32[]{:S(2)}) async-start(bf16[4,128,896]{2,1,0:T(8,128)(2,1)} %broadcast_in_dim.16), calls=%async_computation.5 | async-start | bytes 1835008 | tf_op jit(solution)/shard_map/all_to_all | solution.py:34
  84.8 106.1 %reduce-scatter.6.cloned.1.call-start = ((), (), s32[]{:S(2)}) async-start(), calls=%async_computation.19 | async-start | bytes 2228224 | tf_op jit(solution)/shard_map/reduce_scatter | solution.py:122
  110.5 3.4 copy-start.6
  113.9 1.9 copy-start.12
  113.9 2.1 copy-start.4
  157.0 18.8 %all-to-all-start.3 = ((bf16[8,2,8,4096]{3,2,1,0:T(8,128)(2,1)}), bf16[8,2,8,4096]{3,2,1,0:T(8,128)(2,1)S(1)}, u32[]{:S(2)}, u32[]{:S(2)}) async-start(bf16[8,2,8,4096]{3,2,1,0:T(8,128)(2,1)} %broadcast_in_dim.15), calls=%async_computation.3 | async-start | bytes 2097152 | tf_op jit(solution)/shard_map/all_to_all | solution.py:34
  192.5 11.8 %all-to-all-start.6 = ((bf16[8,128,64]{1,2,0:T(8,128)(2,1)}), bf16[8,128,64]{1,2,0:T(8,128)(2,1)S(1)}, u32[]{:S(2)}, u32[]{:S(2)}) async-start(bf16[8,128,64]{1,2,0:T(8,128)(2,1)} %copy_bitcast_fusion.2), calls=%async_computation.8 | async-start | bytes 262144 | tf_op jit(solution)/shard_map/all_to_all | solution.py:128
  199.1 151.6 %all-gather.2.cloned.1.call-start = ((), (), s32[]{:S(2)}) async-start(), calls=%async_computation.21 | async-start | bytes 2359296 | tf_op jit(solution)/shard_map/all_gather | solution.py:90
  209.0 146.7 %reduce-scatter.8.cloned.1.call-start = ((), (), s32[]{:S(2)}) async-start(), calls=%async_computation.20 | async-start | bytes 8257536 | tf_op jit(solution)/shard_map/reduce_scatter | solution.py:180
  245.4 14.6 %copy-start.5 = (bf16[448,4096]{1,0:T(8,128)(2,1)S(1)}, bf16[448,4096]{1,0:T(8,128)(2,1)}, u32[]{:S(2)}) copy-start(bf16[448,4096]{1,0:T(8,128)(2,1)} %param.14) | copy-start | bytes 11010052
  245.4 14.6 %copy-start.13 = (f32[128,448]{0,1:T(8,128)S(1)}, f32[128,448]{0,1:T(8,128)}, u32[]{:S(2)}) copy-start(f32[128,448]{0,1:T(8,128)} %copy-done.12) | copy-start | bytes 688132
  245.4 14.6 %copy-start.14 = (f32[128,448]{0,1:T(8,128)S(1)}, f32[128,448]{0,1:T(8,128)}, u32[]{:S(2)}) copy-start(f32[128,448]{0,1:T(8,128)} %get-tuple-element.42) | copy-start | bytes 688132
  266.3 3.1 copy-start.7
  271.3 17.7 %all-to-all-start.13 = ((bf16[16,128,256]{2,1,0:T(8,128)(2,1)}), bf16[16,128,256]{2,1,0:T(8,128)(2,1)}, u32[]{:S(2)}, u32[]{:S(2)}) async-start(bf16[16,128,256]{2,1,0:T(8,128)(2,1)} %bitcast.108), calls=%async_computation.16 | async-start | bytes 2097152 | tf_op jit(solution)/shard_map/all_to_all | solution.py:53
  289.0 30.0 %all-to-all-start.12 = ((bf16[128,8,512]{0,2,1:T(8,128)(2,1)}), bf16[128,8,512]{0,2,1:T(8,128)(2,1)S(1)}, u32[]{:S(2)}, u32[]{:S(2)}) async-start(bf16[128,8,512]{0,2,1:T(8,128)(2,1)} %bitcast.110), calls=%async_computation.15 | async-start | bytes 2097152 | tf_op jit(solution)/shard_map/all_to_all | solution.py:171
  319.6 9.8 %all-to-all-start.14 = ((f32[16,128,1]{1,2,0:T(1,128)}), f32[16,128,1]{1,2,0:T(1,128)S(1)}, u32[]{:S(2)}, u32[]{:S(2)}) async-start(f32[16,128,1]{1,2,0:T(1,128)} %broadcast_in_dim.20), calls=%async_computation.17 | async-start | bytes 16384 | tf_op jit(solution)/shard_map/all_to_all | solution.py:34
  329.4 21.3 %all-to-all-start.11 = ((bf16[8,128,512]{2,1,0:T(8,128)(2,1)}), bf16[8,128,512]{2,1,0:T(8,128)(2,1)}, u32[]{:S(2)}, u32[]{:S(2)}) async-start(bf16[8,128,512]{2,1,0:T(8,128)(2,1)} %fusion.9), calls=%async_computation.14 | async-start | bytes 2097152 | tf_op jit(solution)/shard_map/all_to_all | solution.py:173
  338.7 15.2 %copy-start.8 = (bf16[8,128,512]{2,1,0:T(8,128)(2,1)S(1)}, bf16[8,128,512]{2,1,0:T(8,128)(2,1)}, u32[]{:S(2)}) copy-start(bf16[8,128,512]{2,1,0:T(8,128)(2,1)} %copy.61) | copy-start | bytes 3145732
  350.7 3.1 copy-start.10
  353.8 5.3 %copy-start.1 = (bf16[1024,1024]{1,0:T(8,128)(2,1)S(1)}, bf16[1024,1024]{1,0:T(8,128)(2,1)}, u32[]{:S(2)}) copy-start(bf16[1024,1024]{1,0:T(8,128)(2,1)} %param.16) | copy-start | bytes 6291460
  (2 other events, 2.2 us)
Sparse Core Ops, SparseCore 0:
  40.2 37.1 reduce-scatter.3
  110.0 80.8 reduce-scatter.5
  209.2 23.2 all-gather.1
  266.4 57.8 reduce-scatter.7
